TPU v7x, 256 devices: a whole 4x4x8 slice. The times are simulated.
256 devices in a mesh: dp: 32 (over z, y_hi, core), owner: 8 (over y_lo, x).
Axes of the slice: x: 4, y: 4 (y_hi: 2, y_lo: 2; y = y_hi * 2 + y_lo), z: 8, core: 2. Of those that a mesh axis runs over, the one named last changes fastest.
Arguments:
- hidden: bfloat16 [4096, 4096], P('dp'), may hold values from -6 to 6
- norm_gain: float32 [4096], replicated, may hold values from 0.3 to 3
- cotangent: bfloat16 [4096, 6144], P('dp'), may hold values from -30 to 30
Outputs:
- update: bfloat16 [6144, 4096], P('dp', 'owner')
All inputs are finite; a program needn't handle non-finite values. Where the computation divides by a largest or mean magnitude, that divisor is 1e-20 or more.
Results may differ from a plain program's by a relative error of at most 0.014.
Values may be sent and summed in bfloat16 or wider, within the bound.
No kernel may reach another device: no remote copies, remote signals or barrier semaphores. Data moves between devices by JAX's collectives and lax.ppermute only.
A program may use at most 128 MiB of HBM per device.

v0:
```python
import functools
import jax
import jax.numpy as jnp
from jax import lax
from jax.sharding import Mesh
from jax.sharding import PartitionSpec as P

TILE = 1024
OWNER = ("owner_0", "owner_1")
DP = ("dp_0", "dp_1", "dp_2")
DP_OWNER = ("dp_0", "dp_1", "dp_2", "owner_0", "owner_1")
DAMPING = 0.1


def padded_to(lines, length):
    spare = -lines.shape[0] % length
    if not spare:
        return lines
    return jnp.concatenate([lines, jnp.zeros((spare, *lines.shape[1:]), lines.dtype)])


def sum_in_two_steps(shard, axis):
    lines = shard.reshape(-1, *shard.shape[1:][-1:])
    own = lax.psum_scatter(
        padded_to(lines, lax.axis_size(axis)), axis, scatter_dimension=0, tiled=True
    )
    whole = lax.all_gather(own, axis).reshape(-1, *lines.shape[1:])
    return lax.slice_in_dim(whole, 0, len(lines)).reshape(shard.shape)


def over_axes(shard, axes):
    return functools.reduce(lax.psum, axes, shard)


def shards(hidden, norm_gain, cotangent):
    owners = lax.axis_size(OWNER)
    position = lax.axis_index(OWNER)
    groups = lax.axis_size(DP)
    tokens_here = hidden.shape[0]
    width = hidden.shape[1]
    out_width = cotangent.shape[1]
    blocks_all = (width + out_width) // TILE
    slots = (blocks_all + owners - 1) // owners
    states = hidden.astype(jnp.float32)
    normed = (
        states * lax.rsqrt(jnp.mean(states * states, axis=1, keepdims=True) + 1e-05) * norm_gain
    ).astype(jnp.bfloat16)
    source = jnp.concatenate([normed, cotangent], axis=1)
    columns = []
    for slot in range(slots):
        block = jnp.minimum(position + slot * owners, blocks_all - 1)
        columns.append(lax.dynamic_slice_in_dim(source, block * TILE, TILE, 1))
    pieces = jnp.stack(columns)
    partial_value = jnp.einsum("stk,stl->skl", pieces, pieces, preferred_element_type=jnp.float32)
    identity = jnp.eye(TILE, dtype=jnp.float32)
    factor = sum_in_two_steps(partial_value, DP)
    matrix = factor / (tokens_here * groups) + DAMPING * identity
    scale = 1.0 / jnp.max(jnp.sum(jnp.abs(matrix), axis=2), axis=1)
    first = 2.0 * scale[:, None, None] * identity - (scale * scale)[:, None, None] * matrix
    first_low = first.astype(jnp.bfloat16)
    matrix_low = matrix.astype(jnp.bfloat16)
    product = jnp.einsum(
        "skl,slm->skm", first_low, matrix_low, preferred_element_type=jnp.float32
    ).astype(jnp.bfloat16)
    inverse = (
        2.0 * first
        - jnp.einsum("skl,slm->skm", product, first_low, preferred_element_type=jnp.float32)
    ).astype(jnp.bfloat16)
    precond = jnp.einsum(
        "stk,skl->stl", pieces, inverse, preferred_element_type=jnp.float32
    ).astype(jnp.bfloat16)
    gathered = lax.all_gather(precond[:, None], OWNER, axis=1, tiled=True)
    ordered = gathered.reshape(slots * owners, tokens_here, TILE)[:blocks_all]
    inputs_side = width // TILE
    pre_in = jnp.transpose(ordered[:inputs_side], (1, 0, 2)).reshape(tokens_here, width)
    pre_out = jnp.transpose(ordered[inputs_side:], (1, 0, 2)).reshape(tokens_here, out_width)
    own_rows = width // owners
    mine_in = lax.dynamic_slice_in_dim(pre_in, position * own_rows, own_rows, 1)
    summed = lax.psum_scatter(
        jnp.einsum("tk,tl->kl", pre_out, mine_in, preferred_element_type=jnp.float32).astype(
            jnp.bfloat16
        ),
        DP,
        scatter_dimension=0,
        tiled=True,
    ).astype(jnp.float32)
    squares = over_axes(jnp.sum(summed * summed), DP_OWNER)
    return (summed * lax.rsqrt(squares / (width * out_width) + 1e-06)).astype(jnp.bfloat16)


def solution(mesh):
    split = Mesh(
        mesh.devices.reshape(8, 2, 2, 2, 4), ("dp_0", "dp_1", "dp_2", "owner_0", "owner_1")
    )
    return jax.shard_map(
        shards,
        mesh=split,
        in_specs=(P(DP, None), P(), P(DP, None)),
        out_specs=P(DP, OWNER),
        check_vma=False,
    )
```

profile of v0, /device:TPU:8, one launch (start us, length us, event | category | flops | bytes accessed | tf_op | source)
XLA Modules:
  0.0 577.2 jit_solution(10745259062472830327)
XLA Ops:
  6.5 0.0 reduce-scatter.3.cloned.1.call-start
  6.5 1.5 fusion.10
  8.1 1.6 fusion.12
  9.6 1.3 fusion.19
  10.9 4.5 fusion.16
  15.4 0.0 reduce-scatter.3.cloned.1.call-update
  15.4 0.0 all-gather.5.cloned.1.call-start
  15.5 156.2 %reduce-scatter.3.cloned.1.call-done = f32[64,1024]{1,0:T(8,128)} async-done(((f32[2048,1024]{1,0:T(8,128)}), f32[64,1024]{1,0:T(8,128)}) %reduce-scatter.3.cloned.1.call-update) | async-done | bytes 262160 | tf_op jit(solution)/shard_map/reduce_scatter | solution.py:24
  171.7 0.0 all-gather.5.cloned.1.call-update
  171.7 0.0 all-gather.7.cloned.1.call-start
  171.7 2.4 fusion.6
  174.2 2.5 fusion.5
  176.7 97.3 %all-gather.5.cloned.1.call-done = f32[2048,1024]{1,0:T(8,128)} async-done(((f32[64,1024]{1,0:T(8,128)}), f32[2048,1024]{1,0:T(8,128)}) %all-gather.5.cloned.1.call-update) | async-done | bytes 8388624 | tf_op jit(solution)/shard_map/all_gather | solution.py:27
  273.9 0.0 copy-start.1
  273.9 5.4 broadcast_multiply_fusion
  279.4 0.0 copy-start
  279.4 0.0 copy-done.1
  279.4 4.7 add.64
  284.1 1.0 copy-done
  285.1 4.3 abs_reduce_fusion
  289.4 0.1 reduce_max.10
  289.5 0.1 reduce_max.14
  289.6 0.1 reduce_max.18
  289.7 24.7 %fusion.2 = f32[2,1024,1024]{2,1,0:T(8,128)} fusion(f32[2,1024,1024]{2,1,0:T(8,128)} %bitcast.17, f32[1024,1024]{1,0:T(8,128)} %fusion.6, f32[2]{0:T(128)S(1)} %mul.104, f32[1024,1024]{1,0:T(8,128)} %fusion.5, f32[2]{0:T(128)S(1)} %get-tuple-element.5), kind=kOutput, calls=%fused_computation.8 | convolution fusion | flops 8617197568 | bytes 25165840 | tf_op jit(solution)/shard_map/skl,slm->skm/dot_general | solution.py:67
  314.5 10.4 %fusion.13 = bf16[2,128,1024]{2,1,0:T(8,128)(2,1)} fusion(f32[2,1024,1024]{2,1,0:T(8,128)} %fusion.2, f32[2,1024,1024]{2,1,0:T(8,128)} %bitcast.18, f32[2]{0:T(128)S(1)} %mul.104, f32[1024,1024]{1,0:T(8,128)} %fusion.5, f32[2]{0:T(128)S(1)} %get-tuple-element.5, f32[1024,1024]{1,0:T(8,128)} %fusion.6, bf16[1,128,1024]{2,1,0:T(8,128)(2,1)S(1)} %get-tuple-element.8, ...), kind=kOutput, calls=%fused_computation.24 | convolution fusion | flops 552075264 | bytes 26214416 | tf_op jit(solution)/shard_map/stk,skl->stl/dot_general | solution.py:69
  324.8 0.0 all-gather.7.cloned.1.call-update
  324.9 0.2 reduce-scatter.5.cloned.1.call-start
  325.1 51.5 %all-gather.7.cloned.1.call-done = bf16[2,1024,1024]{2,1,0:T(8,128)(2,1)} async-done(((bf16[2,128,1024]{2,1,0:T(8,128)(2,1)}), bf16[2,1024,1024]{2,1,0:T(8,128)(2,1)}) %all-gather.7.cloned.1.call-update) | async-done | bytes 4194320 | tf_op jit(solution)/shard_map/all_gather | solution.py:72
  376.6 1.5 slice.11
  378.1 2.3 slice.12
  380.4 0.9 copy.12
  381.3 1.6 copy.13
  382.9 4.5 convolution_convert_fusion
  387.4 0.0 reduce-scatter.5.cloned.1.call-update
  387.4 135.9 %reduce-scatter.5.cloned.1.call-done = bf16[192,512]{1,0:T(8,128)(2,1)} async-done(((bf16[6144,512]{1,0:T(8,128)(2,1)}), bf16[192,512]{1,0:T(8,128)(2,1)}) %reduce-scatter.5.cloned.1.call-update) | async-done | bytes 196624 | tf_op jit(solution)/shard_map/reduce_scatter | solution.py:79
  523.3 1.6 fusion.14
  524.9 16.6 %psum.35 = f32[]{:T(128)} all-reduce(f32[]{:T(128)} %fusion.14), channel_id=1, replica_groups=mesh['dp_0'=8,'dp_1'=2,'dp_2'=2,'owner_0'=2,'owner_1'=4] {'dp_0'}, use_global_device_ids=true, to_apply=%region_7.0 | all-reduce | flops 1 | bytes 8 | tf_op jit(solution)/shard_map/psum | solution.py:32
  541.5 7.1 %psum.36 = f32[]{:T(128)} all-reduce(f32[]{:T(128)} %psum.35), channel_id=1, replica_groups=mesh['dp_0'=8,'dp_1'=2,'dp_2'=2,'owner_0'=2,'owner_1'=4] {'dp_1'}, use_global_device_ids=true, to_apply=%region_8.0 | all-reduce | flops 1 | bytes 8 | tf_op jit(solution)/shard_map/psum | solution.py:32
  548.6 3.1 psum.37
  551.7 5.6 psum.38
  557.2 11.1 %psum.39 = f32[]{:T(128)} all-reduce(f32[]{:T(128)} %psum.38), channel_id=1, replica_groups=mesh['dp_0'=8,'dp_1'=2,'dp_2'=2,'owner_0'=2,'owner_1'=4] {'owner_1'}, use_global_device_ids=true, to_apply=%region_11.12 | all-reduce | flops 1 | bytes 8 | tf_op jit(solution)/shard_map/psum | solution.py:32
  569.0 1.6 fusion.15
  (3 shorter events, 0.0 us)
Async XLA Ops:
  6.5 165.1 %reduce-scatter.3.cloned.1.call-start = ((), (), s32[]{:S(2)}) async-start(), calls=%async_computation.2 | async-start | bytes 8650752 | tf_op jit(solution)/shard_map/reduce_scatter | solution.py:24
  15.4 258.5 %all-gather.5.cloned.1.call-start = ((), (), s32[]{:S(2)}) async-start(), calls=%async_computation.4 | async-start | bytes 8650752 | tf_op jit(solution)/shard_map/all_gather | solution.py:27
  171.7 204.9 %all-gather.7.cloned.1.call-start = ((), (), s32[]{:S(2)}) async-start(), calls=%async_computation.5 | async-start | bytes 4718592 | tf_op jit(solution)/shard_map/all_gather | solution.py:72
  273.9 5.5 copy-start.1
  279.4 5.7 copy-start
  324.9 198.4 %reduce-scatter.5.cloned.1.call-start = ((), (), s32[]{:S(2)}) async-start(), calls=%async_computation.3 | async-start | bytes 6488064 | tf_op jit(solution)/shard_map/reduce_scatter | solution.py:79
Sparse Core Ops, SparseCore 0:
  15.6 156.0 reduce-scatter.2
  174.5 99.4 all-gather.4
  325.0 51.5 all-gather.6
  387.5 135.7 reduce-scatter.4
where the time goes:
time: 578 us; the launch traced here: 577 us
  waiting for transfers between devices  441 us (76%)
  matrix products  44.1 us (8%)
  blocking collectives  43.4 us (8%)
  other arithmetic  22.5 us (4%)
  between operations  13.9 us (2%)
  local copies, waits for them, and re-layouts  12.1 us (2%)
    reduce_scatter x1, waiting for transfers between devices, sum_in_two_steps(): lax.psum_scatter(padded_to(lines, lax.axis_size(axis)), axis, scatter_dim...  156 us
    reduce_scatter x1, waiting for transfers between devices, shards(): lax.psum_scatter(jnp.einsum('tk,tl->kl', pre_out, mine_in, preferred_elem...  136 us
    all_gather x1, waiting for transfers between devices, sum_in_two_steps(): whole = lax.all_gather(own, axis).reshape(-1, *lines.shape[1:])  97.3 us
    all_gather x1, waiting for transfers between devices, shards(): gathered = lax.all_gather(precond[:, None], OWNER, axis=1, tiled=True)  51.5 us
    psum x5, blocking collectives, over_axes(): return functools.reduce(lax.psum, axes, shard)  43.4 us
    dot_general x1, matrix products, shards(): jnp.einsum('skl,slm->skm', product, first_low, preferred_element_type=jnp...  24.7 us
  transfers between devices with their start and end apart: 4, of which 4 were waited for; matrix products, arithmetic and copies ran while one was open for 1% of the time, Pallas kernels for 0%

commit v1 on v0

--- a/solution.py
+++ b/solution.py
@@ -69,7 +69,9 @@
     precond = jnp.einsum(
         "stk,skl->stl", pieces, inverse, preferred_element_type=jnp.float32
     ).astype(jnp.bfloat16)
-    gathered = lax.all_gather(precond[:, None], OWNER, axis=1, tiled=True)
+    own_2 = precond[:, None]
+    sent = jnp.stack([own_2] * lax.axis_size(OWNER))
+    gathered = jnp.concatenate(lax.all_to_all(sent, OWNER, 0, 0), axis=1)
     ordered = gathered.reshape(slots * owners, tokens_here, TILE)[:blocks_all]
     inputs_side = width // TILE
     pre_in = jnp.transpose(ordered[:inputs_side], (1, 0, 2)).reshape(tokens_here, width)

time: 578 us -> 592 us (1.024)
  waiting for transfers between devices: 441 us -> 449 us
    all_gather x1 -> x0, waiting for transfers between devices: 51.5 us -> none  [shards(): gathered = lax.all_gather(precond[:, None], OWNER, axis=1, tiled=True)]
    all_to_all x0 -> x1, waiting for transfers between devices: none -> 48.7 us  [shards(): gathered = jnp.concatenate(lax.all_to_all(sent, OWNER, 0, 0), axis=1)]
    reduce_scatter x1, waiting for transfers between devices: 136 us -> 147 us  [shards(): lax.psum_scatter(jnp.einsum('tk,tl->kl', pre_out, mine_in, preferred_elem...]
where the time goes in v1:
time: 592 us
  waiting for transfers between devices  449 us (76%)
  matrix products  43.3 us (7%)
  blocking collectives  43.3 us (7%)
  other arithmetic  21.7 us (4%)
  local copies, waits for them, and re-layouts  14.6 us (2%)
  between operations  13.9 us (2%)
  starting transfers between devices  5.92 us (1%)
    reduce_scatter x1, waiting for transfers between devices, sum_in_two_steps(): lax.psum_scatter(padded_to(lines, lax.axis_size(axis)), axis, scatter_dim...  156 us
    reduce_scatter x1, waiting for transfers between devices, shards(): lax.psum_scatter(jnp.einsum('tk,tl->kl', pre_out, mine_in, preferred_elem...  147 us
    all_gather x1, waiting for transfers between devices, sum_in_two_steps(): whole = lax.all_gather(own, axis).reshape(-1, *lines.shape[1:])  97.3 us
    all_to_all x1, waiting for transfers between devices, shards(): gathered = jnp.concatenate(lax.all_to_all(sent, OWNER, 0, 0), axis=1)  48.7 us
    psum x5, blocking collectives, over_axes(): return functools.reduce(lax.psum, axes, shard)  43.3 us
    dot_general x1, matrix products, shards(): jnp.einsum('skl,slm->skm', product, first_low, preferred_element_type=jnp...  24.7 us
  transfers between devices with their start and end apart: 4, of which 4 were waited for; matrix products, arithmetic and copies ran while one was open for 1% of the time, Pallas kernels for 0%

profile of v1, /device:TPU:8, one launch (start us, length us, event | category | flops | bytes accessed | tf_op | source)
XLA Modules:
  0.0 591.8 jit_solution(17079609428639322440)
XLA Ops:
  6.5 0.0 copy-start.2
  6.5 0.0 reduce-scatter.3.cloned.1.call-start
  6.5 1.6 fusion.10
  8.2 1.6 fusion.12
  9.7 0.0 copy-done.2
  9.8 0.3 fusion.19
  10.1 4.5 fusion.16
  14.6 0.0 reduce-scatter.3.cloned.1.call-update
  14.6 0.0 all-gather.3.cloned.1.call-start
  14.7 156.3 %reduce-scatter.3.cloned.1.call-done = f32[64,1024]{1,0:T(8,128)} async-done(((f32[2048,1024]{1,0:T(8,128)}), f32[64,1024]{1,0:T(8,128)}) %reduce-scatter.3.cloned.1.call-update) | async-done | bytes 262160 | tf_op jit(solution)/shard_map/reduce_scatter | solution.py:24
  170.9 0.0 all-gather.3.cloned.1.call-update
  171.0 2.4 fusion.6
  173.4 2.5 fusion.5
  175.9 97.3 %all-gather.3.cloned.1.call-done = f32[2048,1024]{1,0:T(8,128)} async-done(((f32[64,1024]{1,0:T(8,128)}), f32[2048,1024]{1,0:T(8,128)}) %all-gather.3.cloned.1.call-update) | async-done | bytes 8388624 | tf_op jit(solution)/shard_map/all_gather | solution.py:27
  273.2 0.0 copy-start.1
  273.2 5.4 broadcast_multiply_fusion
  278.7 0.0 copy-start
  278.7 0.0 copy-done.1
  278.7 4.7 add.64
  283.4 1.0 copy-done
  284.4 4.3 abs_reduce_fusion
  288.7 0.1 reduce_max.10
  288.8 0.1 reduce_max.14
  288.9 0.1 reduce_max.18
  289.0 24.7 %fusion.2 = f32[2,1024,1024]{2,1,0:T(8,128)} fusion(f32[2,1024,1024]{2,1,0:T(8,128)} %bitcast.19, f32[1024,1024]{1,0:T(8,128)} %fusion.6, f32[2]{0:T(128)S(1)} %mul.104, f32[1024,1024]{1,0:T(8,128)} %fusion.5, f32[2]{0:T(128)S(1)} %get-tuple-element.5), kind=kOutput, calls=%fused_computation.8 | convolution fusion | flops 8617197568 | bytes 25165840 | tf_op jit(solution)/shard_map/skl,slm->skm/dot_general | solution.py:67
  313.8 9.5 %fusion.13 = bf16[2,128,1024]{2,1,0:T(8,128)(2,1)S(1)} fusion(f32[2,1024,1024]{2,1,0:T(8,128)} %fusion.2, f32[2,1024,1024]{2,1,0:T(8,128)} %bitcast.20, f32[2]{0:T(128)S(1)} %mul.104, f32[1024,1024]{1,0:T(8,128)} %fusion.5, f32[2]{0:T(128)S(1)} %get-tuple-element.5, f32[1024,1024]{1,0:T(8,128)} %fusion.6, bf16[1,128,1024]{2,1,0:T(8,128)(2,1)S(1)} %get-tuple-element.8, ...), kind=kOutput, calls=%fused_computation.25 | convolution fusion | flops 552075264 | bytes 26214416 | tf_op jit(solution)/shard_map/stk,skl->stl/dot_general | solution.py:69
  323.3 2.5 stack.15
  325.8 5.9 all-to-all-start
  331.7 0.0 reduce-scatter.5.cloned.1.call-start
  331.7 48.7 %all-to-all-done = bf16[8,2,1,128,1024]{4,3,1,2,0:T(8,128)(2,1)} async-done(((bf16[8,2,1,128,1024]{4,3,1,2,0:T(8,128)(2,1)}), bf16[8,2,1,128,1024]{4,3,1,2,0:T(8,128)(2,1)}, u32[]{:S(2)}, u32[]{:S(2)}) %all-to-all-start) | async-done | bytes 4194336 | tf_op jit(solution)/shard_map/all_to_all | solution.py:74
  380.5 2.6 copy.13
  383.1 0.1 slice_bitcast_fusion
  383.2 1.1 slice_bitcast_fusion.1
  384.3 0.9 copy.14
  385.2 1.6 copy.15
  386.8 4.5 convolution_convert_fusion
  391.3 0.0 reduce-scatter.5.cloned.1.call-update
  391.3 146.6 %reduce-scatter.5.cloned.1.call-done = bf16[192,512]{1,0:T(8,128)(2,1)} async-done(((bf16[6144,512]{1,0:T(8,128)(2,1)}), bf16[192,512]{1,0:T(8,128)(2,1)}) %reduce-scatter.5.cloned.1.call-update) | async-done | bytes 196624 | tf_op jit(solution)/shard_map/reduce_scatter | solution.py:81
  537.9 1.6 fusion.14
  539.5 16.7 %psum.35 = f32[]{:T(128)} all-reduce(f32[]{:T(128)} %fusion.14), channel_id=1, replica_groups=mesh['dp_0'=8,'dp_1'=2,'dp_2'=2,'owner_0'=2,'owner_1'=4] {'dp_0'}, use_global_device_ids=true, to_apply=%region_7.0 | all-reduce | flops 1 | bytes 8 | tf_op jit(solution)/shard_map/psum | solution.py:32
  556.2 7.1 %psum.36 = f32[]{:T(128)} all-reduce(f32[]{:T(128)} %psum.35), channel_id=1, replica_groups=mesh['dp_0'=8,'dp_1'=2,'dp_2'=2,'owner_0'=2,'owner_1'=4] {'dp_1'}, use_global_device_ids=true, to_apply=%region_8.0 | all-reduce | flops 1 | bytes 8 | tf_op jit(solution)/shard_map/psum | solution.py:32
  563.3 3.1 psum.37
  566.4 5.6 psum.38
  571.9 11.0 %psum.39 = f32[]{:T(128)} all-reduce(f32[]{:T(128)} %psum.38), channel_id=1, replica_groups=mesh['dp_0'=8,'dp_1'=2,'dp_2'=2,'owner_0'=2,'owner_1'=4] {'owner_1'}, use_global_device_ids=true, to_apply=%region_11.12 | all-reduce | flops 1 | bytes 8 | tf_op jit(solution)/shard_map/psum | solution.py:32
  583.6 1.6 fusion.15
  (3 shorter events, 0.0 us)
Async XLA Ops:
  6.5 3.2 copy-start.2
  6.5 164.4 %reduce-scatter.3.cloned.1.call-start = ((), (), s32[]{:S(2)}) async-start(), calls=%async_computation.3 | async-start | bytes 8650752 | tf_op jit(solution)/shard_map/reduce_scatter | solution.py:24
  14.6 258.6 %all-gather.3.cloned.1.call-start = ((), (), s32[]{:S(2)}) async-start(), calls=%async_computation.5 | async-start | bytes 8650752 | tf_op jit(solution)/shard_map/all_gather | solution.py:27
  273.2 5.5 copy-start.1
  278.7 5.7 copy-start
  325.8 54.6 %all-to-all-start = ((bf16[8,2,1,128,1024]{4,3,1,2,0:T(8,128)(2,1)}), bf16[8,2,1,128,1024]{4,3,1,2,0:T(8,128)(2,1)}, u32[]{:S(2)}, u32[]{:S(2)}) async-start(bf16[8,2,1,128,1024]{4,3,1,2,0:T(8,128)(2,1)} %stack.15), calls=%async_computation.1 | async-start | bytes 8388608 | tf_op jit(solution)/shard_map/all_to_all | solution.py:74
  331.7 206.2 %reduce-scatter.5.cloned.1.call-start = ((), (), s32[]{:S(2)}) async-start(), calls=%async_computation.4 | async-start | bytes 6488064 | tf_op jit(solution)/shard_map/reduce_scatter | solution.py:81
Sparse Core Ops, SparseCore 0:
  14.7 156.1 reduce-scatter.2
  173.7 99.4 all-gather.2
  391.4 146.4 reduce-scatter.4
